TPU v7x, 32 devices: a whole 2x2x4 slice. The times are simulated.
32 devices in a mesh: space: 8 (over y, x, core), mode: 4 (over z).
Axes of the slice: x: 2, y: 2, z: 4, core: 2. Of those that a mesh axis runs over, the one named last changes fastest.
Arguments:
- start_modes: float32 [256, 24576], P('mode', 'space')
- hessian: bfloat16 [128, 8, 192, 192], P('space'), may hold values from -0.15625 to 0.15625
- block_exponent: int32 [128, 8], P('space'), may hold values from -1 to 1
- col_block: int32 [128, 8], P('space'), may hold values from 0 to 19, as said below
- grain_count: int32 [8], P('space'), may hold values from 384 to 512, as said below
Outputs:
- modes: float32 [256, 24576], P('mode', 'space')
Inputs may be any that keep to these rules, and one draw needn't show every extreme that they name: col_block[b, k] lies between b mod 16 and b mod 16 + 2 * 2; slot 0 is b mod 16 + 2; both ends are reached in every slab. `grain_count`: at most 512 grains a slab, reached by at least one slab.
All inputs are finite; a program needn't handle non-finite values.
Results may differ from a plain program's by a relative error of at most 0.0034.
Values may be sent and summed in bfloat16 or wider, within the bound.
A program may use at most 64 MiB of HBM per device.

v0:
```python
import jax
import jax.numpy as jnp
from jax import lax
from jax.sharding import PartitionSpec as P

HALO_BLOCKS = 2


filter_center = -0.5
filter_half = 1.5


def extended(cells, sides, width):
    for axis, dim in sides:
        count = lax.axis_size(axis)
        head = lax.slice_in_dim(cells, 0, width, axis=dim)
        tail = lax.slice_in_dim(cells, cells.shape[dim] - width, cells.shape[dim], axis=dim)
        cells = jnp.concatenate(
            [
                lax.ppermute(tail, axis, [(i, (i + 1) % count) for i in range(count)]),
                cells,
                lax.ppermute(head, axis, [((i + 1) % count, i) for i in range(count)]),
            ],
            axis=dim,
        )
    return cells


def per_device(start_modes, hessian, block_exponent, col_block, grain_count):
    panel_size, rows_here = start_modes.shape
    slab_blocks, contacts, block_size, _ = hessian.shape
    halo_width = HALO_BLOCKS * block_size
    places = lax.broadcasted_iota(jnp.int32, (rows_here,), 0)
    live = (places < 6 * grain_count[0]).astype(jnp.float32)
    scales = jnp.exp2(block_exponent.astype(jnp.float32)).astype(jnp.bfloat16)

    def operate(vectors_low):
        padded = extended(vectors_low, (("space", 1),), halo_width)
        window = padded.reshape(panel_size, slab_blocks + 2 * HALO_BLOCKS, block_size)
        gathered = jnp.take(window, col_block, axis=1)
        gathered = gathered * scales[None, :, :, None]
        image = jnp.einsum("rkij,prkj->pri", hessian, gathered, preferred_element_type=jnp.float32)
        return image.reshape(panel_size, rows_here)

    start = start_modes * live
    image = operate(start.astype(jnp.bfloat16))
    first = (image - filter_center * start) / filter_half * live
    image = operate(first.astype(jnp.bfloat16))
    second = (2.0 * (image - filter_center * first) / filter_half - start) * live
    my_index = lax.axis_index("mode")
    whole = lax.all_gather(second, "mode", axis=0, tiled=True)
    partial_rows = jnp.dot(
        second, whole.T, precision=lax.Precision.HIGHEST, preferred_element_type=jnp.float32
    )
    summed_rows = lax.psum(partial_rows, "space")
    gram = lax.all_gather(summed_rows, "mode", axis=0, tiled=True)
    lower_factor = jnp.linalg.cholesky(gram)
    identity_matrix = jnp.eye(gram.shape[0], dtype=jnp.float32)
    inverse_factor = jax.scipy.linalg.solve_triangular(lower_factor, identity_matrix, lower=True)
    own_inverse = lax.dynamic_slice_in_dim(inverse_factor, my_index * panel_size, panel_size, 0)
    return jnp.dot(
        own_inverse, whole, precision=lax.Precision.HIGHEST, preferred_element_type=jnp.float32
    )


def solution(mesh):
    return jax.shard_map(
        per_device,
        mesh=mesh,
        in_specs=(
            P("mode", "space"),
            P("space", None, None, None),
            P("space", None),
            P("space", None),
            P("space"),
        ),
        out_specs=P("mode", "space"),
        check_vma=False,
    )
```

profile of v0, /device:TPU:0, one launch (start us, length us, event | category | flops | bytes accessed | tf_op | source)
XLA Modules:
  0.0 278.4 jit_solution(5893356217424159986)
XLA Ops:
  7.2 1.2 multiply_convert_fusion
  8.4 0.5 collective-permute-start
  9.0 2.9 %collective-permute-start.1 = (bf16[64,384]{1,0:T(8,128)(2,1)S(1)}, bf16[64,384]{1,0:T(8,128)(2,1)S(1)}, u32[]{:S(2)}, u32[]{:S(2)}) collective-permute-start(bf16[64,384]{1,0:T(8,128)(2,1)S(1)} %get-tuple-element.27), channel_id=1, source_target_pairs={{4,0},{8,4},{12,8},{16,12},{20,16},{24,20},{28,24},{0,28},{5,1},{9... | collective-permute-start | bytes 147464 | tf_op jit(solution)/shard_map/ppermute | solution.py:22
  11.9 0.7 compare_select_fusion
  12.6 0.7 compare_and_fusion
  13.4 0.7 exponential_convert_fusion
  14.4 0.8 reshape.44
  15.2 0.1 copy.29
  15.3 2.8 gather_fusion
  18.1 11.0 %fusion.10 = f32[64,16,192]{2,0,1:T(8,128)} fusion(bf16[16,8,192,192]{3,2,1,0:T(8,128)(2,1)} %param.8, bf16[16,8,64,192]{3,2,1,0:T(8,128)(2,1)} %bitcast.60, pred[16,8]{1,0:T(8,128)(4,1)S(1)} %copy.26, bf16[16,8]{1,0:T(8,128)(2,1)S(1)} %copy.30), kind=kOutput, calls=%fused_computation.16 | convolution fusion | flops 607125504 | bytes 13369728 | tf_op jit(solution)/shard_map/rkij,prkj->pri/dot_general | solution.py:42
  29.1 1.9 copy.31
  31.0 0.4 reshape.45
  31.5 0.8 collective-permute-start.2
  32.3 1.9 collective-permute-start.3
  34.2 1.8 collective-permute-done.2
  36.0 0.8 pad_maximum_fusion.1
  36.8 1.9 reshape.46
  38.9 2.8 gather_fusion.1
  41.6 11.0 %fusion.11 = f32[64,16,192]{2,0,1:T(8,128)} fusion(bf16[16,8,192,192]{3,2,1,0:T(8,128)(2,1)} %param.8, bf16[16,8,64,192]{3,2,1,0:T(8,128)(2,1)} %bitcast.59, pred[16,8]{1,0:T(8,128)(4,1)S(1)} %copy.26, bf16[16,8]{1,0:T(8,128)(2,1)S(1)} %copy.30), kind=kOutput, calls=%fused_computation.17 | convolution fusion | flops 607125504 | bytes 13369728 | tf_op jit(solution)/shard_map/rkij,prkj->pri/dot_general | solution.py:42
  52.6 1.8 copy.34
  54.4 1.3 reshape.47
  55.7 2.3 subtract_multiply_fusion
  58.0 0.2 all-reduce.3.cloned.1.call-start
  58.2 65.6 %all-gather.2.cloned.1.call-done = f32[256,3072]{1,0:T(8,128)} async-done(((f32[64,3072]{1,0:T(8,128)}), f32[256,3072]{1,0:T(8,128)}) %all-gather.2.cloned.1.call-update) | async-done | bytes 3145744 | tf_op jit(solution)/shard_map/all_gather | solution.py:51
  123.8 5.9 %fusion.33 = f32[64,256]{1,0:T(8,128)} fusion(f32[64,3072]{1,0:T(8,128)} %subtract_multiply_fusion, f32[256,3072]{1,0:T(8,128)} %all-gather.2.cloned.1.call-done), kind=kOutput, calls=%fused_computation.68 | convolution fusion | flops 603979776 | bytes 3997696 | tf_op jit(solution)/shard_map/dot_general | solution.py:52
  129.7 52.0 %all-reduce.3.cloned.1.call-done = f32[64,256]{1,0:T(8,128)} async-done(((f32[64,256]{1,0:T(8,128)}), f32[64,256]{1,0:T(8,128)}) %all-reduce.3.cloned.1.call-update) | async-done | bytes 65552 | tf_op jit(solution)/shard_map/psum | solution.py:55
  181.7 14.1 %all_gather.7 = f32[256,256]{1,0:T(8,128)S(1)} all-gather(f32[64,256]{1,0:T(8,128)} %all-reduce.3.cloned.1.call-done), channel_id=1, replica_groups=mesh['space'=8,'mode'=4] {'mode'}, dimensions={0}, use_global_device_ids=true | all-gather | bytes 327680 | tf_op jit(solution)/shard_map/all_gather | solution.py:56
  195.9 0.8 copy.35
  196.7 1.0 fusion.13
  197.7 0.7 copy-done.3
  198.4 11.7 %cholesky.50 = f32[128,128]{1,0:T(8,128)S(1)} custom-call(f32[128,128]{1,0:T(8,128)S(1)} %cholesky.118), custom_call_target="Cholesky" | custom-call | tf_op jit(solution)/shard_map/jit(cholesky)/cholesky | solution.py:57
  210.1 0.6 select_reduce_fusion.1
  210.8 10.6 %custom-call.15 = f32[1,128,128]{1,2,0:T(8,128)S(1)} custom-call(f32[1,128,128]{2,1,0:T(8,128)} %get-tuple-element.31), custom_call_target="InvertDiagBlocksLowerTriangular" | custom-call | tf_op jit(solution)/shard_map/jit(cholesky)/cholesky | solution.py:57
  221.4 1.0 constant_dynamic-update-slice_fusion
  222.5 1.7 convolution_subtract_fusion.1
  224.2 12.5 %cholesky.105 = f32[128,128]{1,0:T(8,128)S(1)} custom-call(f32[128,128]{1,0:T(8,128)} %convolution_subtract_fusion.1), custom_call_target="Cholesky" | custom-call | tf_op jit(solution)/shard_map/jit(cholesky)/cholesky | solution.py:57
  236.8 0.7 compare_reduce_fusion
  238.8 1.0 select_select_fusion
  239.8 5.2 %while.1 = (s32[]{:T(128)}, f32[256,256]{1,0:T(8,128)S(1)}, s32[2,2]{1,0:T(2,128)S(1)}, f32[2,128,128]{2,1,0:T(8,128)}, s32[]{:T(128)}) while((s32[]{:T(128)}, f32[256,256]{1,0:T(8,128)S(1)}, s32[2,2]{1,0:T(2,128)S(1)}, f32[2,128,128]{2,1,0:T(8,128)}, s32[]{:T(128)}) %tuple.26), condition=%wide.while_cond, body=%wide.while_body.sunk | while | flops 2 | bytes 132705 | solution.py:59
  240.0 0.6 fusion.44
  240.6 1.9 bitcast_dynamic-update-slice_fusion.2
  242.5 0.6 fusion.44
  243.1 1.9 bitcast_dynamic-update-slice_fusion.2
  245.0 21.1 %custom-call.16 = f32[2,128,128]{1,2,0:T(8,128)} custom-call(f32[2,128,128]{2,1,0:T(8,128)} %get-tuple-element.13), custom_call_target="InvertDiagBlocksLowerTriangular" | custom-call | tf_op jit(solution)/shard_map/jit(_solve_triangular)/triangular_solve | solution.py:59
  266.1 1.1 fusion.14
  267.2 0.3 convolution_subtract_fusion
  267.5 1.2 fusion.20
  268.7 2.9 %fusion.17 = f32[64,3072]{1,0:T(8,128)} fusion(f32[256,3072]{1,0:T(8,128)S(1)} %copy-done, s32[]{:T(128)S(6)} %select_n.15, f32[128,256]{1,0:T(8,128)S(1)} %fusion.14, f32[128,256]{1,0:T(8,128)S(1)} %fusion.20), kind=kOutput, calls=%fused_computation.36 | convolution fusion | flops 603996160 | bytes 4194308 | tf_op jit(solution)/shard_map/dot_general | solution.py:61
  (34 shorter events, 0.9 us)
Async XLA Ops:
  6.5 117.3 %all-gather.2.cloned.1.call-start = ((), (), s32[]{:S(2)}) async-start(), calls=%async_computation | async-start | bytes 3932160 | tf_op jit(solution)/shard_map/all_gather | solution.py:51
  8.4 5.9 %collective-permute-start = (bf16[64,384]{1,0:T(8,128)(2,1)S(1)}, bf16[64,384]{1,0:T(8,128)(2,1)S(1)}, u32[]{:S(2)}, u32[]{:S(2)}) collective-permute-start(bf16[64,384]{1,0:T(8,128)(2,1)S(1)} %get-tuple-element.26), channel_id=1, source_target_pairs={{0,4},{4,8},{8,12},{12,16},{16,20},{20,24},{24,28},{28,0},{1,5},{5... | collective-permute-start | bytes 147464 | tf_op jit(solution)/shard_map/ppermute | solution.py:20
  9.0 5.4 %collective-permute-start.1 = (bf16[64,384]{1,0:T(8,128)(2,1)S(1)}, bf16[64,384]{1,0:T(8,128)(2,1)S(1)}, u32[]{:S(2)}, u32[]{:S(2)}) collective-permute-start(bf16[64,384]{1,0:T(8,128)(2,1)S(1)} %get-tuple-element.27), channel_id=1, source_target_pairs={{4,0},{8,4},{12,8},{16,12},{20,16},{24,20},{28,24},{0,28},{5,1},{9... | collective-permute-start | bytes 147464 | tf_op jit(solution)/shard_map/ppermute | solution.py:22
  29.1 2.3 copy-start.1
  31.5 4.5 %collective-permute-start.2 = (bf16[64,384]{1,0:T(8,128)(2,1)S(1)}, bf16[64,384]{1,0:T(8,128)(2,1)S(1)}, u32[]{:S(2)}, u32[]{:S(2)}) collective-permute-start(bf16[64,384]{1,0:T(8,128)(2,1)S(1)} %get-tuple-element.24), channel_id=1, source_target_pairs={{0,4},{4,8},{8,12},{12,16},{16,20},{20,24},{24,28},{28,0},{1,5},{5... | collective-permute-start | bytes 147464 | tf_op jit(solution)/shard_map/ppermute | solution.py:20
  32.3 3.7 %collective-permute-start.3 = (bf16[64,384]{1,0:T(8,128)(2,1)S(1)}, bf16[64,384]{1,0:T(8,128)(2,1)S(1)}, u32[]{:S(2)}, u32[]{:S(2)}) collective-permute-start(bf16[64,384]{1,0:T(8,128)(2,1)S(1)} %get-tuple-element.25), channel_id=1, source_target_pairs={{4,0},{8,4},{12,8},{16,12},{20,16},{24,20},{28,24},{0,28},{5,1},{9... | collective-permute-start | bytes 147464 | tf_op jit(solution)/shard_map/ppermute | solution.py:22
  58.0 123.8 %all-reduce.3.cloned.1.call-start = ((), (), s32[]{:S(2)}) async-start(), calls=%async_computation.1 | async-start | bytes 131072 | tf_op jit(solution)/shard_map/psum | solution.py:55
  123.8 144.9 %copy-start = (f32[256,3072]{1,0:T(8,128)S(1)}, f32[256,3072]{1,0:T(8,128)}, u32[]{:S(2)}) copy-start(f32[256,3072]{1,0:T(8,128)} %all-gather.2.cloned.1.call-done) | copy-start | bytes 9437188
  197.7 0.7 copy-start.3
  236.8 2.0 copy-start.2
Sparse Core Ops, SparseCore 0:
  58.1 65.6 all-gather.1
  129.8 51.8 all-reduce.2
where the time goes:
time: 279 us; the launch traced here: 278 us
  waiting for transfers between devices  119 us (43%)
  other arithmetic  65.9 us (24%)
  matrix products  36 us (13%)
  local copies, waits for them, and re-layouts  20.9 us (7%)
  between operations  15.5 us (6%)
  blocking collectives  14.1 us (5%)
  starting transfers between devices  6.4 us (2%)
    all_gather x1, waiting for transfers between devices, per_device(): whole = lax.all_gather(second, 'mode', axis=0, tiled=True)  65.6 us
    psum x1, waiting for transfers between devices, per_device(): summed_rows = lax.psum(partial_rows, 'space')  52 us
    another operation x6, other arithmetic, per_device(): lower_factor = jnp.linalg.cholesky(gram)  36.3 us
    another operation x3, other arithmetic, per_device(): jax.scipy.linalg.solve_triangular(lower_factor, identity_matrix, lower=True)  22.1 us
    dot_general x2, matrix products, operate(): jnp.einsum('rkij,prkj->pri', hessian, gathered, preferred_element_type=jn...  22 us
    all_gather x1, blocking collectives, per_device(): gram = lax.all_gather(summed_rows, 'mode', axis=0, tiled=True)  14.1 us
    dot_general x1, matrix products, per_device(): jnp.dot(second, whole.T, precision=lax.Precision.HIGHEST, preferred_eleme...  5.88 us
  transfers between devices with their start and end apart: 6, of which 3 were waited for; matrix products, arithmetic and copies ran while one was open for 1% of the time, Pallas kernels for 0%

commit v1 on v0

v1 whole, which is shorter than its diff:
```python
import functools

import jax
import jax.numpy as jnp
from jax import lax
from jax.experimental import pallas as pl
from jax.experimental.pallas import tpu as pltpu
from jax.sharding import PartitionSpec as P

HALO_BLOCKS = 2
GROUP = 2

filter_center = -0.5
filter_half = 1.5

F32 = jnp.float32
BF16 = jnp.bfloat16
MESH = pl.DeviceIdType.MESH
HIGHEST = lax.Precision.HIGHEST


def nt_dot(a, b, precision=None):
    return lax.dot_general(
        a, b, (((1,), (1,)), ((), ())), precision=precision, preferred_element_type=F32
    )


def filter_kernel(
    n_space, n_mode, exponent_ref, column_ref, count_ref, start_ref, hessian_ref,
    own_ref, panels_ref, gram_ref,
    hess, start, first, window_a, window_b, gacc, gsend, grecv, gz,
    hess_sem, halo_send, halo_recv, panel_send, panel_recv, rs_send, rs_recv,
    z_send, z_recv, ag_send, ag_recv,
):
    panel_size = start_ref.shape[0]
    slab_blocks, contacts, block, _ = hessian_ref.shape
    groups = slab_blocks // GROUP
    halo = HALO_BLOCKS
    share = panel_size // n_space
    here = lax.axis_index("space")
    level = lax.axis_index("mode")
    right = lax.rem(here + 1, n_space)
    left = lax.rem(here + n_space - 1, n_space)
    above = lax.rem(level + 1, n_mode)

    def hess_copy(b):
        return pltpu.make_async_copy(hessian_ref.at[b], hess.at[b], hess_sem.at[b])

    @pl.loop(0, slab_blocks)
    def _(i):
        hess_copy(lax.rem(i + slab_blocks - GROUP, slab_blocks)).start()

    barrier = pltpu.get_barrier_semaphore()
    for step in range(1, n_space):
        pl.semaphore_signal(barrier, inc=1, device_id={"space": lax.rem(here + step, n_space)}, device_id_type=MESH)
    for step in range(1, n_mode):
        pl.semaphore_signal(barrier, inc=1, device_id={"mode": lax.rem(level + step, n_mode)}, device_id_type=MESH)

    live_count = 6 * count_ref[0]

    def live_of(b):
        places = lax.broadcasted_iota(jnp.int32, (panel_size, block), 1) + b * block
        return (places < live_count).astype(F32)

    for b in range(slab_blocks):
        piece = start_ref[:, b * block:(b + 1) * block] * live_of(b)
        start[b] = piece
        window_a[b + halo] = piece.astype(BF16)

    pl.semaphore_wait(barrier, n_space - 1 + n_mode - 1)

    def halo_copies(window, base):
        to_right = pltpu.make_async_remote_copy(
            src_ref=window.at[pl.ds(slab_blocks, halo)], dst_ref=window.at[pl.ds(0, halo)],
            send_sem=halo_send.at[base], recv_sem=halo_recv.at[base],
            device_id={"space": right}, device_id_type=MESH)
        to_left = pltpu.make_async_remote_copy(
            src_ref=window.at[pl.ds(halo, halo)], dst_ref=window.at[pl.ds(slab_blocks + halo, halo)],
            send_sem=halo_send.at[base + 1], recv_sem=halo_recv.at[base + 1],
            device_id={"space": left}, device_id_type=MESH)
        return to_right, to_left

    halo_a = halo_copies(window_a, 0)
    halo_b = halo_copies(window_b, 2)
    for copy in halo_a:
        copy.start()
    for copy in halo_a:
        copy.wait_recv()

    def image_of(window, b):
        total = None
        for k in range(contacts):
            e = exponent_ref[b, k]
            scale = jnp.where(e > 0, F32(2.0), jnp.where(e < 0, F32(0.5), F32(1.0)))
            vec = window[column_ref[b, k]] * scale.astype(BF16)
            term = nt_dot(vec, hess[b, k])
            total = term if total is None else total + term
        return total

    def first_group(i, carry):
        c = lax.rem(i + groups - 1, groups)
        for half in range(GROUP):
            b = c * GROUP + half
            hess_copy(b).wait()
            piece = (image_of(window_a, b) - filter_center * start[b]) * (1.0 / filter_half) * live_of(b)
            first[b] = piece
            window_b[b + halo] = piece.astype(BF16)
        return carry

    lax.fori_loop(0, 2, first_group, 0)
    for copy in halo_b:
        copy.start()
    lax.fori_loop(2, groups, first_group, 0)

    def panel_copy(q, c):
        return pltpu.make_async_remote_copy(
            src_ref=panels_ref.at[q, c], dst_ref=panels_ref.at[q, c],
            send_sem=panel_send.at[q, c], recv_sem=panel_recv.at[q, c],
            device_id={"mode": above}, device_id_type=MESH)

    has_above = level < n_mode - 1
    gacc[...] = jnp.zeros_like(gacc)

    def second_group(i, carry):
        c = lax.rem(i + 1, groups)
        for half in range(GROUP):
            b = c * GROUP + half
            piece = (2.0 / filter_half * (image_of(window_b, b) - filter_center * first[b]) - start[b]) * live_of(b)
            own_ref[c, :, half * block:(half + 1) * block] = piece
        panels_ref[level, c] = own_ref[c].astype(BF16)

        @pl.when(has_above)
        def _():
            panel_copy(level, c).start()

        whole = own_ref[c]
        gacc[level] += nt_dot(whole, whole, HIGHEST)
        return carry

    for copy in halo_b:
        copy.wait_recv()
    lax.fori_loop(0, groups, second_group, 0)

    for d in range(1, n_mode):
        @pl.when(level >= d)
        def _():
            q = lax.rem(level - d + n_mode, n_mode)

            def arrival(i, carry):
                c = lax.rem(i + 1, groups)
                panel_copy(q, c).wait_recv()

                @pl.when(has_above)
                def _():
                    panel_copy(q, c).start()

                whole = own_ref[c]
                high = whole.astype(BF16)
                low = (whole - high.astype(F32)).astype(BF16)
                other = panels_ref[q, c]
                gacc[q] += nt_dot(high, other) + nt_dot(low, other)
                return carry

            lax.fori_loop(0, groups, arrival, 0)

    for q in range(n_mode):
        for s in range(n_space):
            gsend[s, :, q * panel_size:(q + 1) * panel_size] = gacc[q, s * share:(s + 1) * share, :]

    def rs_copy(target, slot):
        return pltpu.make_async_remote_copy(
            src_ref=gsend.at[target], dst_ref=grecv.at[slot],
            send_sem=rs_send.at[target], recv_sem=rs_recv.at[slot],
            device_id={"space": target}, device_id_type=MESH)

    for step in range(1, n_space):
        rs_copy(lax.rem(here + step, n_space), here).start()
    total = gsend[here]
    for step in range(1, n_space):
        peer = lax.rem(here + step, n_space)
        rs_copy(peer, peer).wait_recv()
        total = total + grecv[peer]
    gz[level] = total

    def z_copy(target, slot):
        return pltpu.make_async_remote_copy(
            src_ref=gz.at[slot], dst_ref=gz.at[slot],
            send_sem=z_send.at[target], recv_sem=z_recv.at[slot],
            device_id={"mode": target}, device_id_type=MESH)

    for step in range(1, n_mode):
        @pl.when(level + step < n_mode)
        def _():
            higher = lax.rem(level + step, n_mode)
            z_copy(higher, level).start()
            gz[higher] = jnp.zeros_like(total)

    for step in range(1, n_mode):
        @pl.when(level >= step)
        def _():
            lower = lax.rem(level - step + n_mode, n_mode)
            z_copy(lower, lower).wait_recv()

    def ag_copy(target, slot):
        return pltpu.make_async_remote_copy(
            src_ref=gz, dst_ref=gram_ref.at[slot],
            send_sem=ag_send.at[target], recv_sem=ag_recv.at[slot],
            device_id={"space": target}, device_id_type=MESH)

    for step in range(1, n_space):
        ag_copy(lax.rem(here + step, n_space), here).start()
    gram_ref[here] = gz[...]
    for step in range(1, n_space):
        peer = lax.rem(here + step, n_space)
        ag_copy(peer, peer).wait_recv()

    for copy in halo_a:
        copy.wait_send()
    for copy in halo_b:
        copy.wait_send()
    for step in range(1, n_space):
        peer = lax.rem(here + step, n_space)
        rs_copy(peer, here).wait_send()
        ag_copy(peer, here).wait_send()
    for step in range(1, n_mode):
        @pl.when(level + step < n_mode)
        def _():
            z_copy(lax.rem(level + step, n_mode), level).wait_send()
    for d in range(n_mode):
        @pl.when(has_above & (level >= d))
        def _():
            q = lax.rem(level - d + n_mode, n_mode)

            def sent(c, carry):
                panel_copy(q, c).wait_send()
                return carry

            lax.fori_loop(0, groups, sent, 0)


def finish_kernel(gram_ref, own_ref, panels_ref, out_ref, scaled, inverse, extra):
    n_mode, groups, panel_size, width = panels_ref.shape
    size = gram_ref.shape[0]
    level = lax.axis_index("mode")
    rows = lax.broadcasted_iota(jnp.int32, (size, size), 0)
    cols = lax.broadcasted_iota(jnp.int32, (size, size), 1)
    eye = (rows == cols).astype(F32)
    edge = (level + 1) * panel_size
    gram = jnp.where(rows < edge, gram_ref[...], eye)
    gram = jnp.where(rows >= cols, gram, 0.0)
    diag_col = jnp.sum(jnp.where(rows == cols, gram, 0.0), axis=1, keepdims=True)
    diag_row = jnp.sum(jnp.where(rows == cols, gram, 0.0), axis=0, keepdims=True)
    scale_col = lax.rsqrt(diag_col)
    scale_row = lax.rsqrt(diag_row)
    lower = jnp.where(rows > cols, gram * scale_col * scale_row, 0.0)
    scaled[...] = lower + lower.T + eye

    def half_lower(error):
        return jnp.where(rows > cols, error, jnp.where(rows == cols, 0.5 * error, 0.0))

    def dot(a, b):
        return jnp.dot(a, b, precision=HIGHEST, preferred_element_type=F32)

    inverse[...] = eye - lower

    def unfinished(state):
        step, worst = state
        return (worst > 1e-3) & (step < 12)

    def improve(state):
        step, _ = state
        x = inverse[...]
        error = nt_dot(dot(x, scaled[...]), x, HIGHEST) - eye
        worst = jnp.max(jnp.abs(error))
        inverse[...] = x - dot(half_lower(error), x)
        return step + 1, jnp.where(worst < 1e30, worst, F32(1e30))

    _, worst = lax.while_loop(unfinished, improve, (0, F32(1.0)))

    @pl.when(jnp.logical_not(worst <= 1e-3))
    def _():
        inverse[...] = eye
        extra[...] = scaled[...]

        def eliminate(j, carry):
            pivot_row = extra[pl.ds(j, 1), :]
            pivot = jnp.sum(jnp.where(lax.broadcasted_iota(jnp.int32, (1, size), 1) == j, pivot_row, 0.0), axis=1, keepdims=True)
            x_row = inverse[pl.ds(j, 1), :]
            column = jnp.sum(jnp.where(cols == j, extra[...], 0.0), axis=1, keepdims=True)
            index = lax.broadcasted_iota(jnp.int32, (size, 1), 0)
            factor = jnp.where(index > j, column / pivot, 0.0)
            extra[...] = extra[...] - factor * pivot_row
            inverse[...] = inverse[...] - factor * x_row
            return carry

        lax.fori_loop(0, size, eliminate, 0)
        pivots = jnp.sum(jnp.where(rows == cols, extra[...], 0.0), axis=1, keepdims=True)
        inverse[...] = inverse[...] * lax.rsqrt(pivots)

    inverse[...] = inverse[...] * scale_row
    mine = inverse[pl.ds(pl.multiple_of(level * panel_size, panel_size), panel_size), :]
    for q in range(n_mode):
        part = mine[:, q * panel_size:(q + 1) * panel_size]

        @pl.when(q == level)
        def _():
            extra[:panel_size, :panel_size] = part

    for c in range(groups):
        out_ref[:, c * width:(c + 1) * width] = dot(extra[:panel_size, :panel_size], own_ref[c])
    for q in range(n_mode - 1):
        @pl.when(q < level)
        def _():
            part = mine[:, q * panel_size:(q + 1) * panel_size].astype(BF16)
            for c in range(groups):
                out_ref[:, c * width:(c + 1) * width] += jnp.dot(part, panels_ref[q, c], preferred_element_type=F32)


def per_device(n_space, n_mode, start_modes, hessian, block_exponent, col_block, grain_count):
    panel_size, rows_here = start_modes.shape
    slab_blocks, contacts, block, _ = hessian.shape
    groups, width = slab_blocks // GROUP, GROUP * block
    share = panel_size // n_space
    modes = panel_size * n_mode
    window = slab_blocks + 2 * HALO_BLOCKS
    vmem = pl.BlockSpec(memory_space=pltpu.VMEM)
    smem = pl.BlockSpec(memory_space=pltpu.SMEM)
    dma = pltpu.SemaphoreType.DMA
    own, panels, gram = pl.pallas_call(
        functools.partial(filter_kernel, n_space, n_mode),
        out_shape=(
            jax.ShapeDtypeStruct((groups, panel_size, width), F32),
            jax.ShapeDtypeStruct((n_mode, groups, panel_size, width), BF16),
            jax.ShapeDtypeStruct((n_space, n_mode, share, modes), F32),
        ),
        in_specs=[smem, smem, smem, vmem, pl.BlockSpec(memory_space=pl.ANY)],
        out_specs=(vmem, vmem, vmem),
        scratch_shapes=[
            pltpu.VMEM(hessian.shape, BF16),
            pltpu.VMEM((slab_blocks, panel_size, block), F32),
            pltpu.VMEM((slab_blocks, panel_size, block), F32),
            pltpu.VMEM((window, panel_size, block), BF16),
            pltpu.VMEM((window, panel_size, block), BF16),
            pltpu.VMEM((n_mode, panel_size, panel_size), F32),
            pltpu.VMEM((n_space, share, modes), F32),
            pltpu.VMEM((n_space, share, modes), F32),
            pltpu.VMEM((n_mode, share, modes), F32),
            dma((slab_blocks,)), dma((4,)), dma((4,)),
            dma((n_mode, groups)), dma((n_mode, groups)),
            dma((n_space,)), dma((n_space,)), dma((n_mode,)), dma((n_mode,)),
            dma((n_space,)), dma((n_space,)),
        ],
        compiler_params=pltpu.CompilerParams(collective_id=0, has_side_effects=True),
        name="filter",
    )(block_exponent, col_block, grain_count, start_modes, hessian)
    gram = jnp.transpose(gram, (1, 0, 2, 3)).reshape(modes, modes)
    return pl.pallas_call(
        finish_kernel,
        out_shape=jax.ShapeDtypeStruct(start_modes.shape, F32),
        in_specs=[vmem, vmem, vmem],
        out_specs=vmem,
        scratch_shapes=[pltpu.VMEM((modes, modes), F32)] * 3,
        name="finish",
    )(gram, own, panels)


def solution(mesh):
    return jax.shard_map(
        functools.partial(per_device, mesh.shape["space"], mesh.shape["mode"]),
        mesh=mesh,
        in_specs=(
            P("mode", "space"),
            P("space", None, None, None),
            P("space", None),
            P("space", None),
            P("space"),
        ),
        out_specs=P("mode", "space"),
        check_vma=False,
    )
```

time: 279 us -> 68.9 us (0.25)
  the two profiles are of different devices: /device:TPU:0 before, /device:TPU:25 now
where the time goes in v1:
time: 68.9 us; the launch traced here: 69.2 us
  Pallas kernels  64.2 us (93%)
  local copies, waits for them, and re-layouts  4.39 us (6%)
    pallas_call x1, Pallas kernels, per_device(): pl.pallas_call(functools.partial(filter_kernel, n_space, n_mode), out_sha...  54.5 us
    pallas_call x1, Pallas kernels, per_device(): pl.pallas_call(finish_kernel, out_shape=jax.ShapeDtypeStruct(start_modes....  9.71 us
    unnamed x2, local copies, waits for them, and re-layouts  2.71 us
    transpose x1, local copies, waits for them, and re-layouts, per_device(): gram = jnp.transpose(gram, (1, 0, 2, 3)).reshape(modes, modes)  1.69 us

profile of v1, /device:TPU:25, one launch (start us, length us, event | category | flops | bytes accessed | tf_op | source)
XLA Modules:
  0.0 69.2 jit_solution(16313682813376244240)
XLA Ops:
  0.7 1.4 %copy.6.exponent_ref = s32[16,8]{1,0:T(8,128)} copy(s32[16,8]{0,1:T(8,128)} %param.7) | data formatting | bytes 1024 | tf_op args[2]
  2.0 1.4 %copy.7.column_ref = s32[16,8]{1,0:T(8,128)} copy(s32[16,8]{0,1:T(8,128)} %param.8) | data formatting | bytes 1024 | tf_op args[3]
  3.4 54.5 %filter.1 = (f32[8,64,384]{2,1,0:T(8,128)}, bf16[4,8,64,384]{3,2,1,0:T(8,128)(2,1)}, f32[8,4,8,256]{3,2,1,0:T(8,128)}) custom-call(s32[16,8]{1,0:T(8,128)} %copy.6.exponent_ref, s32[16,8]{1,0:T(8,128)} %copy.7.column_ref, s32[1]{0:T(128)S(6)} %copy.9.count_ref, f32[64,3072]{1,0:T(8,128)} %start_ref.1, bf16[16,8,192,192]{3,2,1,0:T(8,128)(2,1)} %hessian_ref.1), custom_call_target="tpu_custom_call" | custom-call | tf_op jit(solution)/shard_map/filter/pallas_call | solution.py:329
  57.9 1.7 %copy.8 = f32[4,8,8,256]{3,2,1,0:T(8,128)} copy(f32[4,8,8,256]{3,2,0,1:T(8,128)} %bitcast.3) | data formatting | bytes 524288 | tf_op jit(solution)/shard_map/transpose | solution.py:356
  59.5 9.7 %finish.1 = f32[64,3072]{1,0:T(8,128)} custom-call(f32[256,256]{1,0:T(8,128)} %bitcast.2, f32[8,64,384]{2,1,0:T(8,128)} %get-tuple-element.9.own_ref, bf16[4,8,64,384]{3,2,1,0:T(8,128)(2,1)} %get-tuple-element.10.panels_ref), custom_call_target="tpu_custom_call" | custom-call | tf_op jit(solution)/shard_map/finish/pallas_call | solution.py:357

commit v2 on v1

--- a/solution.py
+++ b/solution.py
@@ -26,11 +26,11 @@
 
 
 def filter_kernel(
-    n_space, n_mode, exponent_ref, column_ref, count_ref, start_ref, hessian_ref,
+    n_space, n_mode, exponent_hbm, column_hbm, count_ref, start_ref, hessian_ref,
     own_ref, panels_ref, gram_ref,
-    hess, start, first, window_a, window_b, gacc, gsend, grecv, gz,
-    hess_sem, halo_send, halo_recv, panel_send, panel_recv, rs_send, rs_recv,
-    z_send, z_recv, ag_send, ag_recv,
+    exponent_ref, column_ref, hess, start, first, window_a, window_b, gacc, gsend, grecv, gz,
+    table_sem, hess_sem, halo_send, halo_recv, panel_send, panel_recv, rs_send, rs_recv,
+    z_send, z_recv, ag_send, ag_recv, down_send, down_recv,
 ):
     panel_size = start_ref.shape[0]
     slab_blocks, contacts, block, _ = hessian_ref.shape
@@ -46,6 +46,13 @@
     def hess_copy(b):
         return pltpu.make_async_copy(hessian_ref.at[b], hess.at[b], hess_sem.at[b])
 
+    tables = (
+        pltpu.make_async_copy(exponent_hbm, exponent_ref, table_sem.at[0]),
+        pltpu.make_async_copy(column_hbm, column_ref, table_sem.at[1]),
+    )
+    for copy in tables:
+        copy.start()
+
     @pl.loop(0, slab_blocks)
     def _(i):
         hess_copy(lax.rem(i + slab_blocks - GROUP, slab_blocks)).start()
@@ -67,6 +74,8 @@
         start[b] = piece
         window_a[b + halo] = piece.astype(BF16)
 
+    for copy in tables:
+        copy.wait()
     pl.semaphore_wait(barrier, n_space - 1 + n_mode - 1)
 
     def halo_copies(window, base):
@@ -119,6 +128,20 @@
             device_id={"mode": above}, device_id_type=MESH)
 
     has_above = level < n_mode - 1
+    top = n_mode - 1
+    early = n_mode >= 3
+    below = lax.rem(level + n_mode - 1, n_mode)
+
+    def down_copy(c):
+        return pltpu.make_async_remote_copy(
+            src_ref=panels_ref.at[top, c], dst_ref=panels_ref.at[top, c],
+            send_sem=down_send.at[c], recv_sem=down_recv.at[c],
+            device_id={"mode": below}, device_id_type=MESH)
+
+    def split(x):
+        high = x.astype(BF16)
+        return high, (x - high.astype(F32)).astype(BF16)
+
     gacc[...] = jnp.zeros_like(gacc)
 
     def second_group(i, carry):
@@ -133,8 +156,13 @@
         def _():
             panel_copy(level, c).start()
 
-        whole = own_ref[c]
-        gacc[level] += nt_dot(whole, whole, HIGHEST)
+        if early:
+            @pl.when(level == top)
+            def _():
+                down_copy(c).start()
+
+        high, low = split(own_ref[c])
+        gacc[level] += nt_dot(high, high) + (nt_dot(high, low) + nt_dot(low, high))
         return carry
 
     for copy in halo_b:
@@ -142,6 +170,8 @@
     lax.fori_loop(0, groups, second_group, 0)
 
     for d in range(1, n_mode):
+        late = early and d == top
+
         @pl.when(level >= d)
         def _():
             q = lax.rem(level - d + n_mode, n_mode)
@@ -154,16 +184,26 @@
                 def _():
                     panel_copy(q, c).start()
 
-                whole = own_ref[c]
-                high = whole.astype(BF16)
-                low = (whole - high.astype(F32)).astype(BF16)
+                high, low = split(own_ref[c])
                 other = panels_ref[q, c]
                 gacc[q] += nt_dot(high, other) + nt_dot(low, other)
                 return carry
 
-            lax.fori_loop(0, groups, arrival, 0)
-
-    for q in range(n_mode):
+            if not late:
+                lax.fori_loop(0, groups, arrival, 0)
+
+    if early:
+        @pl.when(level == top - 1)
+        def _():
+            def meeting(i, carry):
+                c = lax.rem(i + 1, groups)
+                down_copy(c).wait_recv()
+                gacc[n_mode] += nt_dot(panels_ref[top, c], panels_ref[0, c])
+                return carry
+
+            lax.fori_loop(0, groups, meeting, 0)
+
+    for q in range(n_mode + 1):
         for s in range(n_space):
             gsend[s, :, q * panel_size:(q + 1) * panel_size] = gacc[q, s * share:(s + 1) * share, :]
 
@@ -201,6 +241,12 @@
             lower = lax.rem(level - step + n_mode, n_mode)
             z_copy(lower, lower).wait_recv()
 
+    if early:
+        @pl.when(level == top)
+        def _():
+            met = gz[top - 1, :, n_mode * panel_size:]
+            gz[top, :, :panel_size] = gz[top, :, :panel_size] + met
+
     def ag_copy(target, slot):
         return pltpu.make_async_remote_copy(
             src_ref=gz, dst_ref=gram_ref.at[slot],
@@ -214,6 +260,17 @@
         peer = lax.rem(here + step, n_space)
         ag_copy(peer, peer).wait_recv()
 
+    if early:
+        @pl.when(level == top)
+        def _():
+            def landed(i, carry):
+                c = lax.rem(i + 1, groups)
+                panel_copy(0, c).wait_recv()
+                down_copy(c).wait_send()
+                return carry
+
+            lax.fori_loop(0, groups, landed, 0)
+
     for copy in halo_a:
         copy.wait_send()
     for copy in halo_b:
@@ -240,13 +297,18 @@
 
 def finish_kernel(gram_ref, own_ref, panels_ref, out_ref, scaled, inverse, extra):
     n_mode, groups, panel_size, width = panels_ref.shape
-    size = gram_ref.shape[0]
+    n_space, _, share, _ = gram_ref.shape
+    size = n_mode * panel_size
+    for q in range(n_mode):
+        for s in range(n_space):
+            base = q * panel_size + s * share
+            extra[base:base + share, :] = gram_ref[s, q, :, :size]
     level = lax.axis_index("mode")
     rows = lax.broadcasted_iota(jnp.int32, (size, size), 0)
     cols = lax.broadcasted_iota(jnp.int32, (size, size), 1)
     eye = (rows == cols).astype(F32)
     edge = (level + 1) * panel_size
-    gram = jnp.where(rows < edge, gram_ref[...], eye)
+    gram = jnp.where(rows < edge, extra[...], eye)
     gram = jnp.where(rows >= cols, gram, 0.0)
     diag_col = jnp.sum(jnp.where(rows == cols, gram, 0.0), axis=1, keepdims=True)
     diag_row = jnp.sum(jnp.where(rows == cols, gram, 0.0), axis=0, keepdims=True)
@@ -261,7 +323,14 @@
     def dot(a, b):
         return jnp.dot(a, b, precision=HIGHEST, preferred_element_type=F32)
 
-    inverse[...] = eye - lower
+    x = eye - lower
+    low_scaled = scaled[...].astype(BF16)
+    for _ in range(2):
+        low_x = x.astype(BF16)
+        moved = jnp.dot(low_x, low_scaled, preferred_element_type=F32)
+        error = nt_dot(moved.astype(BF16), low_x) - eye
+        x = x - jnp.dot(half_lower(error).astype(BF16), low_x, preferred_element_type=F32)
+    inverse[...] = x
 
     def unfinished(state):
         step, worst = state
@@ -325,35 +394,37 @@
     window = slab_blocks + 2 * HALO_BLOCKS
     vmem = pl.BlockSpec(memory_space=pltpu.VMEM)
     smem = pl.BlockSpec(memory_space=pltpu.SMEM)
+    hbm = pl.BlockSpec(memory_space=pl.ANY)
     dma = pltpu.SemaphoreType.DMA
     own, panels, gram = pl.pallas_call(
         functools.partial(filter_kernel, n_space, n_mode),
         out_shape=(
             jax.ShapeDtypeStruct((groups, panel_size, width), F32),
             jax.ShapeDtypeStruct((n_mode, groups, panel_size, width), BF16),
-            jax.ShapeDtypeStruct((n_space, n_mode, share, modes), F32),
+            jax.ShapeDtypeStruct((n_space, n_mode, share, modes + panel_size), F32),
         ),
-        in_specs=[smem, smem, smem, vmem, pl.BlockSpec(memory_space=pl.ANY)],
+        in_specs=[hbm, hbm, smem, vmem, hbm],
         out_specs=(vmem, vmem, vmem),
         scratch_shapes=[
+            pltpu.SMEM(block_exponent.shape, jnp.int32),
+            pltpu.SMEM(col_block.shape, jnp.int32),
             pltpu.VMEM(hessian.shape, BF16),
             pltpu.VMEM((slab_blocks, panel_size, block), F32),
             pltpu.VMEM((slab_blocks, panel_size, block), F32),
             pltpu.VMEM((window, panel_size, block), BF16),
             pltpu.VMEM((window, panel_size, block), BF16),
-            pltpu.VMEM((n_mode, panel_size, panel_size), F32),
-            pltpu.VMEM((n_space, share, modes), F32),
-            pltpu.VMEM((n_space, share, modes), F32),
-            pltpu.VMEM((n_mode, share, modes), F32),
-            dma((slab_blocks,)), dma((4,)), dma((4,)),
+            pltpu.VMEM((n_mode + 1, panel_size, panel_size), F32),
+            pltpu.VMEM((n_space, share, modes + panel_size), F32),
+            pltpu.VMEM((n_space, share, modes + panel_size), F32),
+            pltpu.VMEM((n_mode, share, modes + panel_size), F32),
+            dma((2,)), dma((slab_blocks,)), dma((4,)), dma((4,)),
             dma((n_mode, groups)), dma((n_mode, groups)),
             dma((n_space,)), dma((n_space,)), dma((n_mode,)), dma((n_mode,)),
-            dma((n_space,)), dma((n_space,)),
+            dma((n_space,)), dma((n_space,)), dma((groups,)), dma((groups,)),
         ],
         compiler_params=pltpu.CompilerParams(collective_id=0, has_side_effects=True),
         name="filter",
     )(block_exponent, col_block, grain_count, start_modes, hessian)
-    gram = jnp.transpose(gram, (1, 0, 2, 3)).reshape(modes, modes)
     return pl.pallas_call(
         finish_kernel,
         out_shape=jax.ShapeDtypeStruct(start_modes.shape, F32),

time: 68.9 us -> 64.2 us (0.932)
  Pallas kernels: 64.2 us -> 60.6 us
  local copies, waits for them, and re-layouts: 4.39 us -> 2.71 us
    pallas_call x1, Pallas kernels: 54.5 us -> 52.7 us  [per_device(): pl.pallas_call(functools.partial(filter_kernel, n_space, n_mode), out_sha...]
    pallas_call x1, Pallas kernels: 9.71 us -> 7.92 us  [per_device(): pl.pallas_call(finish_kernel, out_shape=jax.ShapeDtypeStruct(start_modes....]
    transpose x1 -> x0, local copies, waits for them, and re-layouts: 1.69 us -> none  [per_device(): gram = jnp.transpose(gram, (1, 0, 2, 3)).reshape(modes, modes)]
where the time goes in v2:
time: 64.2 us; the launch traced here: 64 us
  Pallas kernels  60.6 us (94%)
  local copies, waits for them, and re-layouts  2.71 us (4%)
  between operations  0.66 us (1%)
    pallas_call x1, Pallas kernels, per_device(): pl.pallas_call(functools.partial(filter_kernel, n_space, n_mode), out_sha...  52.7 us
    pallas_call x1, Pallas kernels, per_device(): pl.pallas_call(finish_kernel, out_shape=jax.ShapeDtypeStruct(start_modes....  7.92 us
    unnamed x2, local copies, waits for them, and re-layouts  2.71 us

profile of v2, /device:TPU:25, one launch (start us, length us, event | category | flops | bytes accessed | tf_op | source)
XLA Modules:
  0.0 64.0 jit_solution(4810720467326114022)
XLA Ops:
  0.7 1.4 %copy.6.exponent_hbm = s32[16,8]{1,0:T(8,128)} copy(s32[16,8]{0,1:T(8,128)} %param.7) | data formatting | bytes 1024 | tf_op args[2]
  2.0 1.4 %copy.7.column_hbm = s32[16,8]{1,0:T(8,128)} copy(s32[16,8]{0,1:T(8,128)} %param.8) | data formatting | bytes 1024 | tf_op args[3]
  3.4 52.7 %filter.1 = (f32[8,64,384]{2,1,0:T(8,128)}, bf16[4,8,64,384]{3,2,1,0:T(8,128)(2,1)}, f32[8,4,8,320]{3,2,1,0:T(8,128)}) custom-call(s32[16,8]{1,0:T(8,128)} %copy.6.exponent_hbm, s32[16,8]{1,0:T(8,128)} %copy.7.column_hbm, s32[1]{0:T(128)S(6)} %copy.8.count_ref, f32[64,3072]{1,0:T(8,128)} %start_ref.1, bf16[16,8,192,192]{3,2,1,0:T(8,128)(2,1)} %hessian_ref.1), custom_call_target="tpu_custom_call" | custom-call | tf_op jit(solution)/shard_map/filter/pallas_call | solution.py:399
  56.0 7.9 %finish.1 = f32[64,3072]{1,0:T(8,128)} custom-call(f32[8,4,8,320]{3,2,1,0:T(8,128)} %get-tuple-element.8.gram_ref, f32[8,64,384]{2,1,0:T(8,128)} %get-tuple-element.9.own_ref, bf16[4,8,64,384]{3,2,1,0:T(8,128)(2,1)} %get-tuple-element.10.panels_ref), custom_call_target="tpu_custom_call" | custom-call | tf_op jit(solution)/shard_map/finish/pallas_call | solution.py:428

commit v3 on v2

--- a/solution.py
+++ b/solution.py
@@ -99,9 +99,9 @@
     def image_of(window, b):
         total = None
         for k in range(contacts):
-            e = exponent_ref[b, k]
+            e = exponent_ref[k, b]
             scale = jnp.where(e > 0, F32(2.0), jnp.where(e < 0, F32(0.5), F32(1.0)))
-            vec = window[column_ref[b, k]] * scale.astype(BF16)
+            vec = window[column_ref[k, b]] * scale.astype(BF16)
             term = nt_dot(vec, hess[b, k])
             total = term if total is None else total + term
         return total
@@ -187,21 +187,15 @@
                 high, low = split(own_ref[c])
                 other = panels_ref[q, c]
                 gacc[q] += nt_dot(high, other) + nt_dot(low, other)
+                if early and d == top - 1:
+                    @pl.when(level == top - 1)
+                    def _():
+                        down_copy(c).wait_recv()
+                        gacc[n_mode] += nt_dot(panels_ref[top, c], other)
                 return carry
 
             if not late:
                 lax.fori_loop(0, groups, arrival, 0)
-
-    if early:
-        @pl.when(level == top - 1)
-        def _():
-            def meeting(i, carry):
-                c = lax.rem(i + 1, groups)
-                down_copy(c).wait_recv()
-                gacc[n_mode] += nt_dot(panels_ref[top, c], panels_ref[0, c])
-                return carry
-
-            lax.fori_loop(0, groups, meeting, 0)
 
     for q in range(n_mode + 1):
         for s in range(n_space):
@@ -231,34 +225,33 @@
     for step in range(1, n_mode):
         @pl.when(level + step < n_mode)
         def _():
-            higher = lax.rem(level + step, n_mode)
-            z_copy(higher, level).start()
-            gz[higher] = jnp.zeros_like(total)
-
-    for step in range(1, n_mode):
-        @pl.when(level >= step)
-        def _():
-            lower = lax.rem(level - step + n_mode, n_mode)
-            z_copy(lower, lower).wait_recv()
-
-    if early:
-        @pl.when(level == top)
-        def _():
-            met = gz[top - 1, :, n_mode * panel_size:]
-            gz[top, :, :panel_size] = gz[top, :, :panel_size] + met
-
-    def ag_copy(target, slot):
+            z_copy(lax.rem(level + step, n_mode), level).start()
+
+    def ag_copy(target, origin, slot):
         return pltpu.make_async_remote_copy(
-            src_ref=gz, dst_ref=gram_ref.at[slot],
-            send_sem=ag_send.at[target], recv_sem=ag_recv.at[slot],
+            src_ref=gz.at[slot], dst_ref=gram_ref.at[origin, slot],
+            send_sem=ag_send.at[target, slot], recv_sem=ag_recv.at[origin, slot],
             device_id={"space": target}, device_id_type=MESH)
 
-    for step in range(1, n_space):
-        ag_copy(lax.rem(here + step, n_space), here).start()
-    gram_ref[here] = gz[...]
-    for step in range(1, n_space):
-        peer = lax.rem(here + step, n_space)
-        ag_copy(peer, peer).wait_recv()
+    def spread(slot):
+        for step in range(1, n_space):
+            ag_copy(lax.rem(here + step, n_space), here, slot).start()
+        gram_ref[here, slot] = gz[slot]
+
+    spread(level)
+    for q in range(n_mode - 1):
+        @pl.when(q < level)
+        def _():
+            z_copy(q, q).wait_recv()
+            spread(q)
+
+    for q in range(n_mode):
+        @pl.when(q <= level)
+        def _():
+            for step in range(1, n_space):
+                peer = lax.rem(here + step, n_space)
+                ag_copy(peer, peer, q).wait_recv()
+                ag_copy(peer, here, q).wait_send()
 
     if early:
         @pl.when(level == top)
@@ -278,7 +271,6 @@
     for step in range(1, n_space):
         peer = lax.rem(here + step, n_space)
         rs_copy(peer, here).wait_send()
-        ag_copy(peer, here).wait_send()
     for step in range(1, n_mode):
         @pl.when(level + step < n_mode)
         def _():
@@ -299,11 +291,19 @@
     n_mode, groups, panel_size, width = panels_ref.shape
     n_space, _, share, _ = gram_ref.shape
     size = n_mode * panel_size
+    level = lax.axis_index("mode")
     for q in range(n_mode):
         for s in range(n_space):
             base = q * panel_size + s * share
             extra[base:base + share, :] = gram_ref[s, q, :, :size]
-    level = lax.axis_index("mode")
+
+    if n_mode >= 3:
+        @pl.when(level == n_mode - 1)
+        def _():
+            for s in range(n_space):
+                base = size - panel_size + s * share
+                extra[base:base + share, :panel_size] += gram_ref[s, n_mode - 2, :, size:]
+
     rows = lax.broadcasted_iota(jnp.int32, (size, size), 0)
     cols = lax.broadcasted_iota(jnp.int32, (size, size), 1)
     eye = (rows == cols).astype(F32)
@@ -332,6 +332,13 @@
         x = x - jnp.dot(half_lower(error).astype(BF16), low_x, preferred_element_type=F32)
     inverse[...] = x
 
+    def split(a):
+        high = a.astype(BF16)
+        return high, (a - high.astype(F32)).astype(BF16)
+
+    def dot3(a, b, product=functools.partial(jnp.dot, preferred_element_type=F32)):
+        return product(a[0], b[0]) + (product(a[0], b[1]) + product(a[1], b[0]))
+
     def unfinished(state):
         step, worst = state
         return (worst > 1e-3) & (step < 12)
@@ -339,9 +346,10 @@
     def improve(state):
         step, _ = state
         x = inverse[...]
-        error = nt_dot(dot(x, scaled[...]), x, HIGHEST) - eye
+        parts = split(x)
+        error = dot3(split(dot3(parts, split(scaled[...]))), parts, nt_dot) - eye
         worst = jnp.max(jnp.abs(error))
-        inverse[...] = x - dot(half_lower(error), x)
+        inverse[...] = x - dot3(split(half_lower(error)), parts)
         return step + 1, jnp.where(worst < 1e30, worst, F32(1e30))
 
     _, worst = lax.while_loop(unfinished, improve, (0, F32(1.0)))
@@ -406,8 +414,8 @@
         in_specs=[hbm, hbm, smem, vmem, hbm],
         out_specs=(vmem, vmem, vmem),
         scratch_shapes=[
-            pltpu.SMEM(block_exponent.shape, jnp.int32),
-            pltpu.SMEM(col_block.shape, jnp.int32),
+            pltpu.SMEM((contacts, slab_blocks), jnp.int32),
+            pltpu.SMEM((contacts, slab_blocks), jnp.int32),
             pltpu.VMEM(hessian.shape, BF16),
             pltpu.VMEM((slab_blocks, panel_size, block), F32),
             pltpu.VMEM((slab_blocks, panel_size, block), F32),
@@ -420,11 +428,11 @@
             dma((2,)), dma((slab_blocks,)), dma((4,)), dma((4,)),
             dma((n_mode, groups)), dma((n_mode, groups)),
             dma((n_space,)), dma((n_space,)), dma((n_mode,)), dma((n_mode,)),
-            dma((n_space,)), dma((n_space,)), dma((groups,)), dma((groups,)),
+            dma((n_space, n_mode)), dma((n_space, n_mode)), dma((groups,)), dma((groups,)),
         ],
         compiler_params=pltpu.CompilerParams(collective_id=0, has_side_effects=True),
         name="filter",
-    )(block_exponent, col_block, grain_count, start_modes, hessian)
+    )(block_exponent.T, col_block.T, grain_count, start_modes, hessian)
     return pl.pallas_call(
         finish_kernel,
         out_shape=jax.ShapeDtypeStruct(start_modes.shape, F32),

time: 64.2 us -> 58.1 us (0.905)
  Pallas kernels: 60.6 us -> 57.2 us
  local copies, waits for them, and re-layouts: 2.71 us -> 0 us
    unnamed x2 -> x0, local copies, waits for them, and re-layouts: 2.71 us -> none
    pallas_call x1, Pallas kernels: 52.7 us -> 50.3 us  [per_device(): pl.pallas_call(functools.partial(filter_kernel, n_space, n_mode), out_sha...]
    pallas_call x1, Pallas kernels: 7.92 us -> 6.93 us  [per_device(): pl.pallas_call(finish_kernel, out_shape=jax.ShapeDtypeStruct(start_modes....]
where the time goes in v3:
time: 58.1 us; the launch traced here: 57.9 us
  Pallas kernels  57.2 us (98%)
  between operations  0.66 us (1%)
    pallas_call x1, Pallas kernels, per_device(): pl.pallas_call(functools.partial(filter_kernel, n_space, n_mode), out_sha...  50.3 us
    pallas_call x1, Pallas kernels, per_device(): pl.pallas_call(finish_kernel, out_shape=jax.ShapeDtypeStruct(start_modes....  6.93 us

profile of v3, /device:TPU:25, one launch (start us, length us, event | category | flops | bytes accessed | tf_op | source)
XLA Modules:
  0.0 57.9 jit_solution(11345417320873891533)
XLA Ops:
  0.7 50.3 %filter.1 = (f32[8,64,384]{2,1,0:T(8,128)}, bf16[4,8,64,384]{3,2,1,0:T(8,128)(2,1)}, f32[8,4,8,320]{3,2,1,0:T(8,128)}) custom-call(s32[8,16]{1,0:T(8,128)} %bitcast.2, s32[8,16]{1,0:T(8,128)} %bitcast.3, s32[1]{0:T(128)S(6)} %copy.6.count_ref, f32[64,3072]{1,0:T(8,128)} %start_ref.1, bf16[16,8,192,192]{3,2,1,0:T(8,128)(2,1)} %hessian_ref.1), custom_call_target="tpu_custom_call" | custom-call | tf_op jit(solution)/shard_map/filter/pallas_call | solution.py:407
  51.0 6.9 %finish.1 = f32[64,3072]{1,0:T(8,128)} custom-call(f32[8,4,8,320]{3,2,1,0:T(8,128)} %get-tuple-element.8.gram_ref, f32[8,64,384]{2,1,0:T(8,128)} %get-tuple-element.9.own_ref, bf16[4,8,64,384]{3,2,1,0:T(8,128)(2,1)} %get-tuple-element.10.panels_ref), custom_call_target="tpu_custom_call" | custom-call | tf_op jit(solution)/shard_map/finish/pallas_call | solution.py:436

commit v4 on v3

--- a/solution.py
+++ b/solution.py
@@ -287,7 +287,13 @@
             lax.fori_loop(0, groups, sent, 0)
 
 
-def finish_kernel(gram_ref, own_ref, panels_ref, out_ref, scaled, inverse, extra):
+def finish_kernel(gram_ref, own_hbm, panels_hbm, out_ref, scaled, inverse, extra, own_ref, panels_ref, load_sem):
+    loads = (
+        pltpu.make_async_copy(own_hbm, own_ref, load_sem.at[0]),
+        pltpu.make_async_copy(panels_hbm, panels_ref, load_sem.at[1]),
+    )
+    for copy in loads:
+        copy.start()
     n_mode, groups, panel_size, width = panels_ref.shape
     n_space, _, share, _ = gram_ref.shape
     size = n_mode * panel_size
@@ -320,9 +326,6 @@
     def half_lower(error):
         return jnp.where(rows > cols, error, jnp.where(rows == cols, 0.5 * error, 0.0))
 
-    def dot(a, b):
-        return jnp.dot(a, b, precision=HIGHEST, preferred_element_type=F32)
-
     x = eye - lower
     low_scaled = scaled[...].astype(BF16)
     for _ in range(2):
@@ -383,8 +386,11 @@
         def _():
             extra[:panel_size, :panel_size] = part
 
+    for copy in loads:
+        copy.wait()
+    own_part = split(extra[:panel_size, :panel_size])
     for c in range(groups):
-        out_ref[:, c * width:(c + 1) * width] = dot(extra[:panel_size, :panel_size], own_ref[c])
+        out_ref[:, c * width:(c + 1) * width] = dot3(own_part, split(own_ref[c]))
     for q in range(n_mode - 1):
         @pl.when(q < level)
         def _():
@@ -436,9 +442,13 @@
     return pl.pallas_call(
         finish_kernel,
         out_shape=jax.ShapeDtypeStruct(start_modes.shape, F32),
-        in_specs=[vmem, vmem, vmem],
+        in_specs=[vmem, hbm, hbm],
         out_specs=vmem,
-        scratch_shapes=[pltpu.VMEM((modes, modes), F32)] * 3,
+        scratch_shapes=[pltpu.VMEM((modes, modes), F32)] * 3 + [
+            pltpu.VMEM(own.shape, F32),
+            pltpu.VMEM(panels.shape, BF16),
+            dma((2,)),
+        ],
         name="finish",
     )(gram, own, panels)
 

time: 58.1 us -> 57.1 us (0.983)
  Pallas kernels: 57.2 us -> 56.2 us
    pallas_call x1, Pallas kernels: 6.93 us -> 5.89 us  [per_device(): pl.pallas_call(finish_kernel, out_shape=jax.ShapeDtypeStruct(start_modes....]
where the time goes in v4:
time: 57.1 us; the launch traced here: 56.9 us
  Pallas kernels  56.2 us (98%)
  between operations  0.66 us (1%)
    pallas_call x1, Pallas kernels, per_device(): pl.pallas_call(functools.partial(filter_kernel, n_space, n_mode), out_sha...  50.3 us
    pallas_call x1, Pallas kernels, per_device(): pl.pallas_call(finish_kernel, out_shape=jax.ShapeDtypeStruct(start_modes....  5.89 us

profile of v4, /device:TPU:25, one launch (start us, length us, event | category | flops | bytes accessed | tf_op | source)
XLA Modules:
  0.0 56.9 jit_solution(14084604201659779846)
XLA Ops:
  0.7 50.3 %filter.1 = (f32[8,64,384]{2,1,0:T(8,128)}, bf16[4,8,64,384]{3,2,1,0:T(8,128)(2,1)}, f32[8,4,8,320]{3,2,1,0:T(8,128)}) custom-call(s32[8,16]{1,0:T(8,128)} %bitcast.2, s32[8,16]{1,0:T(8,128)} %bitcast.3, s32[1]{0:T(128)S(6)} %copy.6.count_ref, f32[64,3072]{1,0:T(8,128)} %start_ref.1, bf16[16,8,192,192]{3,2,1,0:T(8,128)(2,1)} %hessian_ref.1), custom_call_target="tpu_custom_call" | custom-call | tf_op jit(solution)/shard_map/filter/pallas_call | solution.py:413
  51.0 5.9 %finish.1 = f32[64,3072]{1,0:T(8,128)} custom-call(f32[8,4,8,320]{3,2,1,0:T(8,128)} %get-tuple-element.8.gram_ref, f32[8,64,384]{2,1,0:T(8,128)} %get-tuple-element.9.own_hbm, bf16[4,8,64,384]{3,2,1,0:T(8,128)(2,1)} %get-tuple-element.10.panels_hbm), custom_call_target="tpu_custom_call" | custom-call | tf_op jit(solution)/shard_map/finish/pallas_call | solution.py:442
